TPU v7x, 32 devices: a whole 2x2x4 slice. The times are simulated.
32 devices in a mesh: store: 8 (over z, y), tensor: 4 (over x, core).
Axes of the slice: x: 2, y: 2, z: 4, core: 2. Of those that a mesh axis runs over, the one named last changes fastest.
Arguments:
- tokens: bfloat16 [8192, 8192], P('store', 'tensor'), may hold values from -1200 to 1200
- norm_gain: float32 [8192], P('tensor'), may hold values from 0.1 to 1.9
- kv_weight: bfloat16 [8192, 2, 1024], P('tensor'), may hold values from -0.0625 to 0.0625
- adapter_down: bfloat16 [32, 8192, 128], P('store', 'tensor'), may hold values from -0.0625 to 0.0625
- adapter_up: bfloat16 [32, 2, 64, 1024], P('store', None, None, 'tensor'), may hold values from -0.75 to 0.75
- token_adapters: int32 [8192, 1], P('store'), may hold values from 0 to 31; in each aligned block of 1024 rows (0 to 1023, 1024 to 2047, ...) at most 40 rows name the same one
- adapter_slot: int32 [32], replicated, may hold values from 0 to 31, each once
- request_lengths: int32 [16], replicated, may hold values from 1 to 4096, 8192 in all
Outputs:
- new_keys: bfloat16 [8192, 1024], P('store', 'tensor')
- new_values: bfloat16 [8192, 1024], P('store', 'tensor')
Inputs may be any that keep to these rules, and one draw needn't show every extreme that they name: `token_adapters`: among the 1024 tokens of one index of store no adapter is named more than 40 times; in every draw some adapter is named exactly 40 times by the tokens of some index. `adapter_slot`: each row 0 to 31 appears once. `request_lengths`: the lengths sum to 8192; the largest is exactly 4096.
All inputs are finite; a program needn't handle non-finite values.
Results may differ from a plain program's by a relative error of at most 0.0061.
Values may be sent and summed in bfloat16 or wider, within the bound.
A program may use at most 128 MiB of HBM per device.

v0:
```python
import math

import jax
import jax.numpy as jnp
from jax import lax
from jax.sharding import PartitionSpec as P

D = 8192
HEAD = 128
ADAPTER_RANK = 64


epsilon = 1e-05
adapter_scale = 2.0
rope_theta = 500000.0


def place_rows(adapter_ids, adapter_slot, capacity):
    catalog = jnp.arange(adapter_slot.shape[0], dtype=jnp.int32)
    slot_rows = jnp.sum(
        jnp.where(adapter_ids[:, None] == catalog[None, :], adapter_slot[None, :], 0), axis=1
    )
    row_order = jnp.arange(adapter_ids.shape[0], dtype=jnp.int32)
    same_earlier = (adapter_ids[:, None] == adapter_ids[None, :]) & (
        row_order[None, :] < row_order[:, None]
    )
    rank_rows = jnp.sum(same_earlier.astype(jnp.int32), axis=1)
    return slot_rows * capacity + rank_rows


def positions_of(first_row, row_count, lengths):
    global_rows = first_row + jnp.arange(row_count, dtype=jnp.int32)
    request_ends = jnp.cumsum(lengths)
    preceding = jnp.sum(
        jnp.where(request_ends[None, :] <= global_rows[:, None], lengths[None, :], 0), axis=1
    )
    return global_rows - preceding


def rotate(states, positions):
    per_head = states.reshape(states.shape[0], -1, HEAD)
    half_size = HEAD // 2
    frequency = jnp.exp(
        jnp.arange(half_size, dtype=jnp.float32) * (-2.0 * math.log(rope_theta) / HEAD)
    )
    angles = positions.astype(jnp.float32)[:, None] * frequency[None, :]
    cos_part = jnp.concatenate([jnp.cos(angles), jnp.cos(angles)], axis=1)[:, None, :]
    sin_part = jnp.concatenate([jnp.sin(angles), jnp.sin(angles)], axis=1)[:, None, :]
    low_half = per_head[..., :half_size]
    high_half = per_head[..., half_size:]
    turned = jnp.concatenate([-high_half, low_half], axis=-1)
    return (per_head * cos_part + turned * sin_part).reshape(states.shape)


def local(
    tokens,
    norm_gain,
    kv_weight,
    adapter_down,
    adapter_up,
    token_adapters,
    adapter_slot,
    request_lengths,
):
    row_count = tokens.shape[0]
    local_width = tokens.shape[1]
    adapter_total = adapter_slot.shape[0]
    capacity = max(2, 5 * row_count // (4 * adapter_total))
    store_size = lax.axis_size("store")
    per_owner = adapter_down.shape[0]
    kv_local = adapter_up.shape[3]
    widened = tokens.astype(jnp.float32)
    squares = lax.psum(jnp.sum(widened * widened, axis=1), "tensor")
    normed = (widened * lax.rsqrt(squares / D + epsilon)[:, None] * norm_gain[None, :]).astype(
        jnp.bfloat16
    )
    targets = place_rows(token_adapters[:, 0], adapter_slot, capacity)
    send_rows = (
        jnp.zeros((adapter_total * capacity, local_width), jnp.bfloat16).at[targets].set(normed)
    )
    send_rows = send_rows.reshape(store_size, per_owner, capacity, local_width)
    down_projected = jnp.einsum(
        "slcd,ldr->slcr",
        lax.all_to_all(send_rows, "store", split_axis=0, concat_axis=0, tiled=True),
        adapter_down,
        preferred_element_type=jnp.float32,
    )
    rank_total_sum = lax.psum(down_projected, "tensor")
    rank_activation = (rank_total_sum * adapter_scale).astype(jnp.bfloat16)
    split_rank = rank_activation.reshape(rank_activation.shape[:3] + (2, ADAPTER_RANK))
    update_rows = jnp.einsum(
        "slcjr,ljrk->slcjk", split_rank, adapter_up, preferred_element_type=jnp.float32
    )
    back_rows = update_rows.astype(jnp.bfloat16).reshape(
        rank_activation.shape[:3] + (2 * kv_local,)
    )
    returned = lax.all_to_all(back_rows, "store", split_axis=0, concat_axis=0, tiled=True)
    delta_rows = returned.reshape(adapter_total * capacity, 2, kv_local)[targets]
    partial_value = jnp.einsum("td,djk->tjk", normed, kv_weight, preferred_element_type=jnp.float32)
    base_part = lax.psum_scatter(partial_value, "tensor", scatter_dimension=2, tiled=True)
    combined = base_part + delta_rows.astype(jnp.float32)
    positions = positions_of(lax.axis_index("store") * row_count, row_count, request_lengths)
    new_keys = rotate(combined[:, 0, :], positions).astype(jnp.bfloat16)
    new_values = combined[:, 1, :].astype(jnp.bfloat16)
    return (new_keys, new_values)


def solution(mesh):
    return jax.shard_map(
        local,
        mesh=mesh,
        in_specs=(
            P("store", "tensor"),
            P("tensor"),
            P("tensor", None, None),
            P("store", "tensor", None),
            P("store", None, None, "tensor"),
            P("store", None),
            P(),
            P(),
        ),
        out_specs=(P("store", "tensor"), P("store", "tensor")),
        check_vma=False,
    )
```

profile of v0, /device:TPU:17, one launch (start us, length us, event | category | flops | bytes accessed | tf_op | source)
XLA Modules:
  0.0 276.9 jit_solution(12801032871038219586)
XLA Ops:
  7.2 1.4 convert_reduce_fusion
  9.4 3.1 %fusion = f32[1024]{0:T(1024)S(1)} fusion(bf16[1024,2048]{1,0:T(8,128)(2,1)} %param.8), kind=kLoop, calls=%fused_computation.4 | loop fusion | flops 6290432 | bytes 4198400 | tf_op jit(solution)/shard_map/reduce_sum | solution.py:73
  12.5 5.7 %psum.14 = f32[1024]{0:T(1024)S(1)} all-reduce(f32[1024]{0:T(1024)S(1)} %fusion), channel_id=1, replica_groups=mesh['store'=8,'tensor'=4] {'tensor'}, use_global_device_ids=true, to_apply=%region_1.0 | all-reduce | flops 1024 | bytes 8192 | tf_op jit(solution)/shard_map/psum | solution.py:73
  18.2 11.2 %scatter_custom_fusion = bf16[1280,2048]{1,0:T(8,128)(2,1)} fusion(s32[1024]{0:T(1024)S(1)} %bitcast.50, bf16[]{:T(256)} %constant.6.clone.1, bf16[1024,2048]{1,0:T(8,128)(2,1)} %param.8, f32[2048]{0:T(1024)S(1)} %copy-done.6, f32[1024]{0:T(1024)S(1)} %add_rsqrt_fusion), kind=kCustom, calls=%fused_computation.15 | custom fusion | flops 8388608 | bytes 9449474 | tf_op jit(solution)/shard_map/scatter | solution.py:79
  29.4 118.9 %all_to_all.10 = bf16[8,4,40,2048]{3,2,1,0:T(8,128)(2,1)S(1)} all-to-all(bf16[8,4,40,2048]{3,2,1,0:T(8,128)(2,1)} %bitcast.46), channel_id=1, replica_groups=mesh['store'=8,'tensor'=4] {'store'}, dimensions={0} | all-to-all | bytes 10485760 | tf_op jit(solution)/shard_map/all_to_all | solution.py:84
  148.3 2.5 fusion.13
  151.1 14.9 %fusion.3 = f32[1024,2,1024]{2,0,1:T(8,128)} fusion(bf16[2048,2,1024]{2,1,0:T(2,128)(2,1)} %param.10, bf16[1024,2048]{1,0:T(8,128)(2,1)} %param.8, f32[2048]{0:T(1024)S(1)} %copy-done.6, f32[1024]{0:T(1024)S(1)} %add_rsqrt_fusion), kind=kOutput, calls=%fused_computation.7 | convolution fusion | flops 8598323200 | bytes 20983808 | tf_op jit(solution)/shard_map/td,djk->tjk/dot_general | solution.py:99
  166.0 19.6 %all-reduce.2.cloned.1.call-done = f32[8,4,40,128]{3,2,0,1:T(8,128)} async-done(((f32[8,4,40,128]{3,2,0,1:T(8,128)}), f32[8,4,40,128]{3,2,0,1:T(8,128)}) %all-reduce.2.cloned.1.call-update) | async-done | bytes 655376 | tf_op jit(solution)/shard_map/psum | solution.py:88
  185.6 1.1 multiply_convert_fusion
  187.6 1.3 copy.28
  188.9 1.7 reshape.97
  190.6 5.5 %all-to-all-start.1 = ((bf16[8,4,40,512]{3,2,1,0:T(8,128)(2,1)}), bf16[8,4,40,512]{3,2,1,0:T(8,128)(2,1)S(1)}, u32[]{:S(2)}, u32[]{:S(2)}) async-start(bf16[8,4,40,512]{3,2,1,0:T(8,128)(2,1)} %reshape.97), calls=%async_computation.2 | async-start | bytes 2621440 | tf_op jit(solution)/shard_map/all_to_all | solution.py:97
  196.5 1.9 multiply_cosine_fusion
  198.4 1.3 pad_maximum_fusion
  199.7 23.6 %all-to-all-done.1 = bf16[8,4,40,512]{3,2,1,0:T(8,128)(2,1)S(1)} async-done(((bf16[8,4,40,512]{3,2,1,0:T(8,128)(2,1)}), bf16[8,4,40,512]{3,2,1,0:T(8,128)(2,1)S(1)}, u32[]{:S(2)}, u32[]{:S(2)}) %all-to-all-start.1) | async-done | bytes 1310752 | tf_op jit(solution)/shard_map/all_to_all | solution.py:97
  223.2 1.2 reshape.98
  224.5 5.5 %gather_fusion = bf16[1024,2,256]{2,1,0:T(2,128)(2,1)S(1)} fusion(bf16[1280,2,256]{2,1,0:T(2,128)(2,1)} %reshape.98, s32[1024]{0:T(1024)S(1)} %broadcast_clamp_fusion), kind=kCustom, calls=%fused_computation | custom fusion | bytes 2101248 | tf_op jit(solution)/shard_map/gather | solution.py:98
  230.0 30.2 %reduce-scatter.2.cloned.1.call-done = f32[1024,2,256]{2,0,1:T(8,128)} async-done(((f32[1024,2,1024]{2,0,1:T(8,128)}), f32[1024,2,256]{2,0,1:T(8,128)}) %reduce-scatter.2.cloned.1.call-update) | async-done | bytes 2097168 | tf_op jit(solution)/shard_map/reduce_scatter | solution.py:100
  260.2 1.8 convert_add_fusion
  262.0 1.1 slice.19
  264.5 1.7 reshape_squeeze.6
  266.3 1.1 slice_negate_fusion
  267.4 1.2 maximum_multiply_fusion
  269.0 1.0 fusion.20
  (36 shorter events, 4.0 us)
Async XLA Ops:
  7.2 141.1 %copy-start = (bf16[4,2048,128]{2,1,0:T(8,128)(2,1)S(1)}, bf16[4,2048,128]{2,1,0:T(8,128)(2,1)}, u32[]{:S(2)}) copy-start(bf16[4,2048,128]{2,1,0:T(8,128)(2,1)} %param.11) | copy-start | bytes 6291460
  7.2 11.0 %copy-start.6 = (f32[2048]{0:T(1024)S(1)}, f32[2048]{0:T(1024)}, u32[]{:S(2)}) copy-start(f32[2048]{0:T(1024)} %param.9) | copy-start | bytes 24580
  7.2 178.4 %all-reduce.2.cloned.1.call-start = ((), (), s32[]{:S(2)}) async-start(), calls=%async_computation.4 | async-start | bytes 1310720 | tf_op jit(solution)/shard_map/psum | solution.py:88
  150.8 109.3 %reduce-scatter.2.cloned.1.call-start = ((), (), s32[]{:S(2)}) async-start(), calls=%async_computation.3 | async-start | bytes 10485760 | tf_op jit(solution)/shard_map/reduce_scatter | solution.py:100
  165.9 21.1 %copy-start.5 = (bf16[4,2,64,256]{3,2,1,0:T(8,128)(2,1)S(1)}, bf16[4,2,64,256]{3,2,1,0:T(8,128)(2,1)}, u32[]{:S(2)}) copy-start(bf16[4,2,64,256]{3,2,1,0:T(8,128)(2,1)} %param.12) | copy-start | bytes 786436
  187.6 8.5 %copy-start.7 = (s32[16]{0:T(128)S(1)}, s32[16]{0:T(128)}, u32[]{:S(2)}) copy-start(s32[16]{0:T(128)} %param.15) | copy-start | bytes 196
  190.6 32.6 %all-to-all-start.1 = ((bf16[8,4,40,512]{3,2,1,0:T(8,128)(2,1)}), bf16[8,4,40,512]{3,2,1,0:T(8,128)(2,1)S(1)}, u32[]{:S(2)}, u32[]{:S(2)}) async-start(bf16[8,4,40,512]{3,2,1,0:T(8,128)(2,1)} %reshape.97), calls=%async_computation.2 | async-start | bytes 2621440 | tf_op jit(solution)/shard_map/all_to_all | solution.py:97
  262.0 1.7 copy-start.1
  266.2 1.2 copy-start.4
  266.2 2.4 copy-start.3
  266.2 2.8 %copy-start.2 = (f32[1024,2,256]{2,0,1:T(8,128)S(1)}, f32[1024,2,256]{2,0,1:T(8,128)}, u32[]{:S(2)}) copy-start(f32[1024,2,256]{2,0,1:T(8,128)} %copy-done.1) | copy-start | bytes 6291460
Sparse Core Ops, SparseCore 0:
  151.0 34.6 all-reduce.1
  188.2 71.9 reduce-scatter.1
where the time goes:
time: 279 us; the launch traced here: 277 us
  blocking collectives  125 us (45%)
  waiting for transfers between devices  73.4 us (26%)
  other arithmetic  26.2 us (9%)
  matrix products  17.9 us (6%)
  local copies, waits for them, and re-layouts  14.8 us (5%)
  between operations  14.2 us (5%)
  starting transfers between devices  5.73 us (2%)
    all_to_all x1, blocking collectives, local(): lax.all_to_all(send_rows, 'store', split_axis=0, concat_axis=0, tiled=True)  119 us
    reduce_scatter x1, waiting for transfers between devices, local(): lax.psum_scatter(partial_value, 'tensor', scatter_dimension=2, tiled=True)  30.2 us
    all_to_all x1, waiting for transfers between devices, local(): lax.all_to_all(back_rows, 'store', split_axis=0, concat_axis=0, tiled=True)  23.6 us
    psum x1, waiting for transfers between devices, local(): rank_total_sum = lax.psum(down_projected, 'tensor')  19.6 us
    dot_general x1, matrix products, local(): jnp.einsum('td,djk->tjk', normed, kv_weight, preferred_element_type=jnp.f...  14.9 us
    scatter x1, other arithmetic, local(): jnp.zeros((adapter_total * capacity, local_width), jnp.bfloat16).at[targets]  11.2 us
    psum x1, blocking collectives, local(): squares = lax.psum(jnp.sum(widened * widened, axis=1), 'tensor')  5.7 us
  transfers between devices with their start and end apart: 3, of which 3 were waited for; matrix products, arithmetic and copies ran while one was open for 11% of the time, Pallas kernels for 0%

commit v1 on v0

--- a/solution.py
+++ b/solution.py
@@ -1,8 +1,11 @@
+import functools
 import math
 
 import jax
 import jax.numpy as jnp
 from jax import lax
+from jax.experimental import pallas as pl
+from jax.experimental.pallas import tpu as pltpu
 from jax.sharding import PartitionSpec as P
 
 D = 8192
@@ -50,6 +53,349 @@
     high_half = per_head[..., half_size:]
     turned = jnp.concatenate([-high_half, low_half], axis=-1)
     return (per_head * cos_part + turned * sin_part).reshape(states.shape)
+
+
+MESH = pl.DeviceIdType.MESH
+
+
+def send_order(size):
+    return sorted(range(1, size), key=lambda step: (abs(2 * step - size), step))
+
+
+def fused_kernel(
+    stores,
+    tensors,
+    tok,
+    gain,
+    trow,
+    tcol,
+    cos_t,
+    sin_t,
+    up,
+    w_hbm,
+    down_hbm,
+    keys_o,
+    vals_o,
+    g,
+    w,
+    down,
+    sq_out,
+    sq_in,
+    snd,
+    rcv,
+    acc,
+    base_out,
+    base_in,
+    low_out,
+    low_in,
+    ret_out,
+    ret_in,
+    load_sem,
+    sq_ss,
+    sq_rs,
+    tok_ss,
+    tok_rs,
+    base_ss,
+    base_rs,
+    low_ss,
+    low_rs,
+    ret_ss,
+    ret_rs,
+):
+    rows, width = tok.shape
+    per_owner = down.shape[0]
+    block = rcv.shape[1]
+    capacity = block // per_owner
+    kv_local = up.shape[3]
+    kv_whole = kv_local * tensors
+    me_s = lax.axis_index("store")
+    me_t = lax.axis_index("tensor")
+
+    load_w = pltpu.make_async_copy(w_hbm, w, load_sem.at[0])
+    load_d = pltpu.make_async_copy(down_hbm, down, load_sem.at[1])
+    load_w.start()
+    load_d.start()
+
+    barrier = pltpu.get_barrier_semaphore()
+    for step in range(1, stores):
+        pl.semaphore_signal(
+            barrier, inc=1, device_id={"store": (me_s + step) % stores}, device_id_type=MESH
+        )
+    for step in range(1, tensors):
+        pl.semaphore_signal(
+            barrier, inc=1, device_id={"tensor": (me_t + step) % tensors}, device_id_type=MESH
+        )
+    pl.semaphore_wait(barrier, stores + tensors - 2)
+
+    def remote(src, dst, ss, rs, axis, target):
+        return pltpu.make_async_remote_copy(
+            src_ref=src, dst_ref=dst, send_sem=ss, recv_sem=rs,
+            device_id={axis: target}, device_id_type=MESH,
+        )
+
+    def to_tensor(step):
+        return (me_t + step) % tensors
+
+    tile = 128
+
+    def scale(i, _):
+        at = pl.ds(pl.multiple_of(i * tile, tile), tile)
+        x = tok[at, :].astype(jnp.float32)
+        g[at, :] = (x * gain[...]).astype(jnp.bfloat16)
+        total = x[:, 0:128] * x[:, 0:128]
+        for lane in range(1, width // 128):
+            part = x[:, lane * 128 : (lane + 1) * 128]
+            total = total + part * part
+        sq_out[at, :] = total
+        return 0
+
+    lax.fori_loop(0, rows // tile, scale, 0)
+
+    sq_copies = [
+        remote(sq_out, sq_in.at[m - 1], sq_ss.at[m - 1], sq_rs.at[m - 1], "tensor", to_tensor(m))
+        for m in range(1, tensors)
+    ]
+
+    chunk = 512
+    order = send_order(stores)
+    tok_copies = {
+        step: remote(
+            snd.at[step - 1], rcv.at[step], tok_ss.at[step], tok_rs.at[step],
+            "store", (me_s + step) % stores,
+        )
+        for step in order
+    }
+
+    def pick(step, dst):
+        places = lax.broadcasted_iota(jnp.int32, (block, rows), 0) + step * block
+        choose = jnp.where(places == trow[...], 1.0, 0.0).astype(jnp.bfloat16)
+
+        def part(i, _):
+            at = pl.ds(pl.multiple_of(i * chunk, chunk), chunk)
+            dst[:, at] = jnp.dot(
+                choose, g[:, at], preferred_element_type=jnp.float32
+            ).astype(jnp.bfloat16)
+            return 0
+
+        lax.fori_loop(0, width // chunk, part, 0)
+
+    for place, step in enumerate(order):
+        pick(step, snd.at[step - 1])
+        if place:
+            tok_copies[order[place - 1]].start()
+    pick(0, rcv.at[0])
+    tok_copies[order[-1]].start()
+    for copy in sq_copies:
+        copy.start()
+
+    load_w.wait()
+    base_copies = [
+        remote(
+            base_out.at[m - 1], base_in.at[m - 1], base_ss.at[m - 1], base_rs.at[m - 1],
+            "tensor", to_tensor(m),
+        )
+        for m in range(1, tensors)
+    ]
+    mt = 256
+    for m in list(range(1, tensors)) + [0]:
+        for j in range(2):
+            cols = pl.ds(
+                pl.multiple_of(j * kv_whole + to_tensor(m) * kv_local, kv_local), kv_local
+            )
+
+            def base(i, _, m=m, j=j, cols=cols):
+                at = pl.ds(pl.multiple_of(i * mt, mt), mt)
+                r = jnp.dot(g[at, :], w[:, cols], preferred_element_type=jnp.float32)
+                if m:
+                    base_out[m - 1, at, j * kv_local : (j + 1) * kv_local] = r.astype(jnp.bfloat16)
+                else:
+                    acc[at, j * kv_local : (j + 1) * kv_local] = r
+                return 0
+
+            lax.fori_loop(0, rows // mt, base, 0)
+        if m > 1:
+            base_copies[m - 2].start()
+        if m == 0:
+            base_copies[tensors - 2].start()
+
+    load_d.wait()
+    owner_of = lax.broadcasted_iota(jnp.int32, (block, 1), 0) // capacity
+    low_copies = {}
+
+    def lower(step):
+        if step:
+            tok_copies[step].wait_recv()
+        x = rcv[step]
+        low = jnp.zeros((block, 128), jnp.float32)
+        for l in range(per_owner):
+            r = jnp.dot(x, down[l], preferred_element_type=jnp.float32)
+            low = jnp.where(owner_of == l, r, low)
+        low_out[step] = low
+        for m in range(1, tensors):
+            low_copies[step, m] = remote(
+                low_out.at[step], low_in.at[m - 1, step], low_ss.at[step, m - 1],
+                low_rs.at[step, m - 1], "tensor", to_tensor(m),
+            )
+            low_copies[step, m].start()
+
+    ret_copies = {}
+
+    def raise_back(step):
+        total = low_out[step]
+        for m in range(1, tensors):
+            low_copies[step, m].wait_recv()
+            total = total + low_in[m - 1, step]
+        middle = (total * adapter_scale).astype(jnp.bfloat16)
+        for j in range(2):
+            mj = middle[:, j * ADAPTER_RANK : (j + 1) * ADAPTER_RANK]
+            d = jnp.zeros((block, kv_local), jnp.float32)
+            for l in range(per_owner):
+                r = jnp.dot(mj, up[l, j], preferred_element_type=jnp.float32)
+                d = jnp.where(owner_of == l, r, d)
+            ret_out[step, :, j * kv_local : (j + 1) * kv_local] = d.astype(jnp.bfloat16)
+        if step:
+            ret_copies[step] = remote(
+                ret_out.at[step], ret_in.at[step], ret_ss.at[step], ret_rs.at[step],
+                "store", (me_s + stores - step) % stores,
+            )
+            ret_copies[step].start()
+
+    steps = [0] + order
+    for place, step in enumerate(steps):
+        lower(step)
+        if place:
+            raise_back(steps[place - 1])
+    raise_back(steps[-1])
+
+    for m in range(tensors - 1):
+        base_copies[m].wait_recv()
+        sq_copies[m].wait_recv()
+
+    def give(step, src):
+        def part(i, _):
+            at = pl.ds(pl.multiple_of(i * mt, mt), mt)
+            places = lax.broadcasted_iota(jnp.int32, (mt, block), 1) + step * block
+            choose = jnp.where(places == tcol[at, :], 1.0, 0.0).astype(jnp.bfloat16)
+            acc[at, :] = acc[at, :] + jnp.dot(choose, src[...], preferred_element_type=jnp.float32)
+            return 0
+
+        lax.fori_loop(0, rows // mt, part, 0)
+
+    for step in steps:
+        if step:
+            ret_copies[step].wait_recv()
+            give(step, ret_in.at[step])
+        else:
+            give(step, ret_out.at[step])
+
+    def finish(i, _):
+        at = pl.ds(pl.multiple_of(i * tile, tile), tile)
+        square = sq_out[at, :]
+        total = acc[at, :]
+        for m in range(tensors - 1):
+            square = square + sq_in[m, at, :]
+            total = total + base_in[m, at, :].astype(jnp.float32)
+        mean = jnp.sum(square, axis=1, keepdims=True) / (width * tensors)
+        total = total * lax.rsqrt(mean + epsilon)
+        c = cos_t[at, :]
+        s = sin_t[at, :]
+        for head in range(kv_local // HEAD):
+            x = total[:, head * HEAD : (head + 1) * HEAD]
+            y = x * c + pltpu.roll(x, HEAD // 2, 1) * s
+            keys_o[at, head * HEAD : (head + 1) * HEAD] = y.astype(jnp.bfloat16)
+        vals_o[at, :] = total[:, kv_local:].astype(jnp.bfloat16)
+        return 0
+
+    lax.fori_loop(0, rows // tile, finish, 0)
+
+    for copy in sq_copies + base_copies:
+        copy.wait_send()
+    for copies in (tok_copies, low_copies, ret_copies):
+        for copy in copies.values():
+            copy.wait_send()
+
+
+def fused(
+    tokens,
+    norm_gain,
+    kv_weight,
+    adapter_down,
+    adapter_up,
+    token_adapters,
+    adapter_slot,
+    request_lengths,
+):
+    rows, width = tokens.shape
+    adapter_total = adapter_slot.shape[0]
+    capacity = max(2, 5 * rows // (4 * adapter_total))
+    stores = lax.axis_size("store")
+    tensors = lax.axis_size("tensor")
+    per_owner, _, _, kv_local = adapter_up.shape
+    block = per_owner * capacity
+    me = lax.axis_index("store")
+    targets = place_rows(token_adapters[:, 0], adapter_slot, capacity)
+    targets = (targets // block + stores - me) % stores * block + targets % block
+    positions = positions_of(me * rows, rows, request_lengths)
+    half = HEAD // 2
+    frequency = jnp.exp(
+        jnp.arange(half, dtype=jnp.float32) * (-2.0 * math.log(rope_theta) / HEAD)
+    )
+    angles = positions.astype(jnp.float32)[:, None] * frequency[None, :]
+    cos_part = jnp.cos(angles)
+    sin_part = jnp.sin(angles)
+    cos_t = jnp.concatenate([cos_part, cos_part], axis=1)
+    sin_t = jnp.concatenate([-sin_part, sin_part], axis=1)
+    ranks = adapter_down.shape[2]
+    vmem = pl.BlockSpec(memory_space=pltpu.VMEM)
+    hbm = pl.BlockSpec(memory_space=pl.ANY)
+    f32, bf16 = jnp.float32, jnp.bfloat16
+    dma = pltpu.SemaphoreType.DMA
+    return pl.pallas_call(
+        functools.partial(fused_kernel, stores, tensors),
+        out_shape=[jax.ShapeDtypeStruct((rows, kv_local), bf16)] * 2,
+        in_specs=[vmem] * 7 + [hbm] * 2,
+        out_specs=[vmem] * 2,
+        scratch_shapes=[
+            pltpu.VMEM((rows, width), bf16),
+            pltpu.VMEM((width, 2 * kv_local * tensors), bf16),
+            pltpu.VMEM((per_owner, width, ranks), bf16),
+            pltpu.VMEM((rows, 128), f32),
+            pltpu.VMEM((tensors - 1, rows, 128), f32),
+            pltpu.VMEM((stores - 1, block, width), bf16),
+            pltpu.VMEM((stores, block, width), bf16),
+            pltpu.VMEM((rows, 2 * kv_local), f32),
+            pltpu.VMEM((tensors - 1, rows, 2 * kv_local), bf16),
+            pltpu.VMEM((tensors - 1, rows, 2 * kv_local), bf16),
+            pltpu.VMEM((stores, block, ranks), f32),
+            pltpu.VMEM((tensors - 1, stores, block, ranks), f32),
+            pltpu.VMEM((stores, block, 2 * kv_local), bf16),
+            pltpu.VMEM((stores, block, 2 * kv_local), bf16),
+            dma((2,)),
+            dma((tensors - 1,)),
+            dma((tensors - 1,)),
+            dma((stores,)),
+            dma((stores,)),
+            dma((tensors - 1,)),
+            dma((tensors - 1,)),
+            dma((stores, tensors - 1)),
+            dma((stores, tensors - 1)),
+            dma((stores,)),
+            dma((stores,)),
+        ],
+        compiler_params=pltpu.CompilerParams(
+            collective_id=0, has_side_effects=True, vmem_limit_bytes=60 * 1024 * 1024
+        ),
+    )(
+        tokens,
+        norm_gain[None, :],
+        targets[None, :],
+        targets[:, None],
+        cos_t,
+        sin_t,
+        adapter_up,
+        kv_weight.reshape(width, -1),
+        adapter_down,
+    )
 
 
 def local(
@@ -106,8 +452,9 @@
 
 
 def solution(mesh):
+    small = mesh.shape["store"] <= 8 and mesh.shape["tensor"] > 1
     return jax.shard_map(
-        local,
+        fused if small else local,
         mesh=mesh,
         in_specs=(
             P("store", "tensor"),

time: 279 us -> 192 us (0.69)
  Pallas kernels: 0 us -> 167 us
  blocking collectives: 125 us -> 0 us
  waiting for transfers between devices: 73.4 us -> 0 us
  other arithmetic: 26.2 us -> 8.21 us
  matrix products: 17.9 us -> 0 us
  between operations: 14.2 us -> 0.7 us
  starting transfers between devices: 5.73 us -> 0 us
    pallas_call x0 -> x1, Pallas kernels: none -> 167 us  [fused(): pl.pallas_call(functools.partial(fused_kernel, stores, tensors), out_shap...]
    all_to_all x1 -> x0, blocking collectives: 119 us -> none  [local(): lax.all_to_all(send_rows, 'store', split_axis=0, concat_axis=0, tiled=True)]
    reduce_scatter x1 -> x0, waiting for transfers between devices: 30.2 us -> none  [local(): lax.psum_scatter(partial_value, 'tensor', scatter_dimension=2, tiled=True)]
    all_to_all x1 -> x0, waiting for transfers between devices: 23.6 us -> none  [local(): lax.all_to_all(back_rows, 'store', split_axis=0, concat_axis=0, tiled=True)]
    psum x1 -> x0, waiting for transfers between devices: 19.6 us -> none  [local(): rank_total_sum = lax.psum(down_projected, 'tensor')]
    dot_general x3 -> x0, matrix products: 17.9 us -> none  [the longest x1 14.9 us: local(): jnp.einsum('td,djk->tjk', normed, kv_weight, preferred_element_type=jnp.f...]
    unnamed x16 -> x3, local copies, waits for them, and re-layouts: 0.57 us -> 13.9 us
    scatter x1 -> x0, other arithmetic: 11.2 us -> none  [local(): jnp.zeros((adapter_total * capacity, local_width), jnp.bfloat16).at[targets]]
  transfers between devices with their start and end apart: 3 -> 0, of which waited for: 3 -> 0; matrix products, arithmetic and copies ran while one was open for 11% -> 0% of each run, Pallas kernels for 0% -> 0%
where the time goes in v1:
time: 192 us; the launch traced here: 191 us
  Pallas kernels  167 us (87%)
  local copies, waits for them, and re-layouts  15 us (8%)
  other arithmetic  8.21 us (4%)
    pallas_call x1, Pallas kernels, fused(): pl.pallas_call(functools.partial(fused_kernel, stores, tensors), out_shap...  167 us
    unnamed x3, local copies, waits for them, and re-layouts  13.9 us

profile of v1, /device:TPU:17, one launch (start us, length us, event | category | flops | bytes accessed | tf_op | source)
XLA Modules:
  0.0 191.2 jit_solution(7072590723596070076)
XLA Ops:
  0.6 1.3 convert_reduce_fusion
  1.9 0.8 select_reduce_fusion
  2.8 0.6 fusion.7.trow
  3.4 0.7 copy.26
  4.2 0.1 reduce
  4.3 0.7 select_reduce_fusion.1
  5.0 0.2 copy.19
  5.3 0.2 copy.21
  5.5 1.3 fusion.5.tcol
  6.8 1.9 fusion.6
  8.7 1.4 pad_maximum_fusion
  10.1 10.1 %copy.27 = bf16[256,8,2,1024]{3,1,2,0:T(8,128)(2,1)} copy(bf16[256,8,2,1024]{3,2,1,0:T(2,128)(2,1)} %bitcast.10) | data formatting | bytes 16777216
  20.2 167.2 %shard_map.95 = (bf16[1024,256]{1,0:T(8,128)(2,1)}, bf16[1024,256]{1,0:T(8,128)(2,1)}) custom-call(bf16[1024,2048]{1,0:T(8,128)(2,1)} %tok.1, f32[1,2048]{1,0:T(1,128)} %bitcast.15, s32[1,1024]{1,0:T(1,128)} %fusion.7.trow, s32[1024,1]{1,0:T(8,128)} %fusion.5.tcol, f32[1024,128]{1,0:T(8,128)} %get-tuple-element.7.cos_t, f32[1024,128]{1,0:T(8,128)} %get-tuple-element.8.sin_t, ...), custom_call_target="tpu_custom_call" | custom-call | tf_op jit(solution)/shard_map/pallas_call | solution.py:353
  187.4 1.9 copy.30
  189.3 1.9 copy.31
  (6 shorter events, 0.1 us)

commit v2 on v1

--- a/solution.py
+++ b/solution.py
@@ -67,16 +67,19 @@
     tensors,
     tok,
     gain,
+    ids,
+    slots,
+    lengths,
+    up,
+    w_hbm,
+    down_hbm,
+    out,
     trow,
     tcol,
     cos_t,
     sin_t,
-    up,
-    w_hbm,
-    down_hbm,
-    keys_o,
-    vals_o,
     g,
+    w3,
     w,
     down,
     sq_out,
@@ -111,7 +114,7 @@
     me_s = lax.axis_index("store")
     me_t = lax.axis_index("tensor")
 
-    load_w = pltpu.make_async_copy(w_hbm, w, load_sem.at[0])
+    load_w = pltpu.make_async_copy(w_hbm, w3, load_sem.at[0])
     load_d = pltpu.make_async_copy(down_hbm, down, load_sem.at[1])
     load_w.start()
     load_d.start()
@@ -151,6 +154,25 @@
 
     lax.fori_loop(0, rows // tile, scale, 0)
 
+    adapters = slots.shape[0]
+    named = jnp.where(
+        lax.broadcasted_iota(jnp.int32, (adapters, rows), 0) == ids[...], 1.0, 0.0
+    )
+    earlier = jnp.where(
+        lax.broadcasted_iota(jnp.int32, (rows, rows), 0)
+        < lax.broadcasted_iota(jnp.int32, (rows, rows), 1),
+        1.0,
+        0.0,
+    ).astype(jnp.bfloat16)
+    counts = jnp.dot(named.astype(jnp.bfloat16), earlier, preferred_element_type=jnp.float32)
+    rank = jnp.sum(named * counts, axis=0, keepdims=True).astype(jnp.int32)
+    slot = jnp.zeros((1, rows), jnp.int32)
+    for a in range(adapters):
+        slot = jnp.where(ids[...] == a, slots[a], slot)
+    owner = slot // per_owner - me_s
+    owner = jnp.where(owner < 0, owner + stores, owner)
+    trow[...] = owner * block + slot % per_owner * capacity + rank
+
     sq_copies = [
         remote(sq_out, sq_in.at[m - 1], sq_ss.at[m - 1], sq_rs.at[m - 1], "tensor", to_tensor(m))
         for m in range(1, tensors)
@@ -189,6 +211,22 @@
         copy.start()
 
     load_w.wait()
+    dt = 128
+    two = lax.broadcasted_iota(jnp.int32, (dt, 2 * dt), 1) - 2 * lax.broadcasted_iota(
+        jnp.int32, (dt, 2 * dt), 0
+    )
+    every = [jnp.where(two == j, 1.0, 0.0).astype(jnp.bfloat16) for j in range(2)]
+
+    def part_kinds(i, _):
+        at = pl.ds(pl.multiple_of(i * dt, dt), dt)
+        x = w3[at].reshape(2 * dt, kv_whole)
+        for j in range(2):
+            w[at, j * kv_whole : (j + 1) * kv_whole] = jnp.dot(
+                every[j], x, preferred_element_type=jnp.float32
+            ).astype(jnp.bfloat16)
+        return 0
+
+    lax.fori_loop(0, width // dt, part_kinds, 0)
     base_copies = [
         remote(
             base_out.at[m - 1], base_in.at[m - 1], base_ss.at[m - 1], base_rs.at[m - 1],
@@ -217,6 +255,29 @@
             base_copies[m - 2].start()
         if m == 0:
             base_copies[tensors - 2].start()
+
+    half = HEAD // 2
+    lane = lax.broadcasted_iota(jnp.int32, (1, HEAD), 1)
+    frequency = jnp.exp(
+        (lane % half).astype(jnp.float32) * (-2.0 * math.log(rope_theta) / HEAD)
+    )
+    sign = jnp.where(lane < half, -1.0, 1.0)
+
+    def tables(i, _):
+        at = pl.ds(pl.multiple_of(i * tile, tile), tile)
+        row = lax.broadcasted_iota(jnp.int32, (tile, HEAD), 0) + (me_s * rows + i * tile)
+        position = row
+        end = 0
+        for r in range(lengths.shape[0]):
+            end = end + lengths[r]
+            position = jnp.where(row >= end, row - end, position)
+        angles = position.astype(jnp.float32) * frequency
+        cos_t[at, :] = jnp.cos(angles)
+        sin_t[at, :] = jnp.sin(angles) * sign
+        tcol[at, :] = jnp.broadcast_to(trow[:, at], (tile, tile)).T
+        return 0
+
+    lax.fori_loop(0, rows // tile, tables, 0)
 
     load_d.wait()
     owner_of = lax.broadcasted_iota(jnp.int32, (block, 1), 0) // capacity
@@ -275,7 +336,7 @@
         def part(i, _):
             at = pl.ds(pl.multiple_of(i * mt, mt), mt)
             places = lax.broadcasted_iota(jnp.int32, (mt, block), 1) + step * block
-            choose = jnp.where(places == tcol[at, :], 1.0, 0.0).astype(jnp.bfloat16)
+            choose = jnp.where(places == tcol[at, 0:1], 1.0, 0.0).astype(jnp.bfloat16)
             acc[at, :] = acc[at, :] + jnp.dot(choose, src[...], preferred_element_type=jnp.float32)
             return 0
 
@@ -302,8 +363,8 @@
         for head in range(kv_local // HEAD):
             x = total[:, head * HEAD : (head + 1) * HEAD]
             y = x * c + pltpu.roll(x, HEAD // 2, 1) * s
-            keys_o[at, head * HEAD : (head + 1) * HEAD] = y.astype(jnp.bfloat16)
-        vals_o[at, :] = total[:, kv_local:].astype(jnp.bfloat16)
+            out[at, head * HEAD : (head + 1) * HEAD] = y.astype(jnp.bfloat16)
+        out[at, kv_local:] = total[:, kv_local:].astype(jnp.bfloat16)
         return 0
 
     lax.fori_loop(0, rows // tile, finish, 0)
@@ -326,37 +387,29 @@
     request_lengths,
 ):
     rows, width = tokens.shape
-    adapter_total = adapter_slot.shape[0]
-    capacity = max(2, 5 * rows // (4 * adapter_total))
+    capacity = max(2, 5 * rows // (4 * adapter_slot.shape[0]))
     stores = lax.axis_size("store")
     tensors = lax.axis_size("tensor")
     per_owner, _, _, kv_local = adapter_up.shape
     block = per_owner * capacity
-    me = lax.axis_index("store")
-    targets = place_rows(token_adapters[:, 0], adapter_slot, capacity)
-    targets = (targets // block + stores - me) % stores * block + targets % block
-    positions = positions_of(me * rows, rows, request_lengths)
-    half = HEAD // 2
-    frequency = jnp.exp(
-        jnp.arange(half, dtype=jnp.float32) * (-2.0 * math.log(rope_theta) / HEAD)
-    )
-    angles = positions.astype(jnp.float32)[:, None] * frequency[None, :]
-    cos_part = jnp.cos(angles)
-    sin_part = jnp.sin(angles)
-    cos_t = jnp.concatenate([cos_part, cos_part], axis=1)
-    sin_t = jnp.concatenate([-sin_part, sin_part], axis=1)
     ranks = adapter_down.shape[2]
     vmem = pl.BlockSpec(memory_space=pltpu.VMEM)
+    smem = pl.BlockSpec(memory_space=pltpu.SMEM)
     hbm = pl.BlockSpec(memory_space=pl.ANY)
     f32, bf16 = jnp.float32, jnp.bfloat16
     dma = pltpu.SemaphoreType.DMA
-    return pl.pallas_call(
+    both = pl.pallas_call(
         functools.partial(fused_kernel, stores, tensors),
-        out_shape=[jax.ShapeDtypeStruct((rows, kv_local), bf16)] * 2,
-        in_specs=[vmem] * 7 + [hbm] * 2,
-        out_specs=[vmem] * 2,
+        out_shape=jax.ShapeDtypeStruct((rows, 2 * kv_local), bf16),
+        in_specs=[vmem] * 3 + [smem] * 2 + [vmem] + [hbm] * 2,
+        out_specs=vmem,
         scratch_shapes=[
+            pltpu.VMEM((1, rows), jnp.int32),
+            pltpu.VMEM((rows, 128), jnp.int32),
+            pltpu.VMEM((rows, HEAD), f32),
+            pltpu.VMEM((rows, HEAD), f32),
             pltpu.VMEM((rows, width), bf16),
+            pltpu.VMEM((width, 2, kv_local * tensors), bf16),
             pltpu.VMEM((width, 2 * kv_local * tensors), bf16),
             pltpu.VMEM((per_owner, width, ranks), bf16),
             pltpu.VMEM((rows, 128), f32),
@@ -388,14 +441,14 @@
     )(
         tokens,
         norm_gain[None, :],
-        targets[None, :],
-        targets[:, None],
-        cos_t,
-        sin_t,
+        token_adapters.reshape(1, rows),
+        adapter_slot,
+        request_lengths,
         adapter_up,
-        kv_weight.reshape(width, -1),
+        kv_weight,
         adapter_down,
     )
+    return both[:, :kv_local], both[:, kv_local:]
 
 
 def local(

time: 192 us -> 170 us (0.89)
  local copies, waits for them, and re-layouts: 15 us -> 2.23 us
  other arithmetic: 8.21 us -> 0 us
    unnamed x3 -> x0, local copies, waits for them, and re-layouts: 13.9 us -> none
    reduce_sum x3 -> x0, other arithmetic: 2.82 us -> none  [the longest x1 1.28 us: place_rows(): rank_rows = jnp.sum(same_earlier.astype(jnp.int32), axis=1)]
    slice x0 -> x1, local copies, waits for them, and re-layouts: none -> 2.23 us  [fused(): return (both[:, :kv_local], both[:, kv_local:])]
    add x3 -> x0, other arithmetic: 1.93 us -> none  [the longest x2 1.93 us: fused(): (targets // block + stores - me) % stores * block + targets % block]
where the time goes in v2:
time: 170 us
  Pallas kernels  167 us (98%)
  local copies, waits for them, and re-layouts  2.23 us (1%)
    pallas_call x1, Pallas kernels, fused(): pl.pallas_call(functools.partial(fused_kernel, stores, tensors), out_shap...  167 us

profile of v2, /device:TPU:17, one launch (start us, length us, event | category | flops | bytes accessed | tf_op | source)
XLA Modules:
  0.0 170.3 jit_solution(1198571080015048534)
XLA Ops:
  0.6 167.4 %shard_map.95 = bf16[1024,512]{1,0:T(8,128)(2,1)} custom-call(bf16[1024,2048]{1,0:T(8,128)(2,1)} %tok.1, f32[1,2048]{1,0:T(1,128)} %bitcast.2, s32[1,1024]{1,0:T(1,128)} %bitcast.3, s32[32]{0:T(128)} %slots.1, s32[16]{0:T(128)} %lengths.1, bf16[4,2,64,256]{3,2,1,0:T(8,128)(2,1)} %up.1, bf16[2048,2,1024]{2,1,0:T(2,128)(2,1)} %w_hbm.1, ...), custom_call_target="tpu_custom_call" | custom-call | tf_op jit(solution)/shard_map/pallas_call | solution.py:401
  168.0 2.2 %fusion = (bf16[1024,256]{1,0:T(8,128)(2,1)}, bf16[1024,256]{1,0:T(8,128)(2,1)}) fusion(bf16[1024,512]{1,0:T(8,128)(2,1)} %shard_map.95), kind=kLoop, calls=%fused_computation | loop fusion | bytes 2097152 | tf_op jit(solution)/shard_map/slice | solution.py:451

commit v3 on v2

--- a/solution.py
+++ b/solution.py
@@ -78,6 +78,7 @@
     tcol,
     cos_t,
     sin_t,
+    scale_t,
     g,
     w3,
     w,
@@ -321,17 +322,6 @@
             )
             ret_copies[step].start()
 
-    steps = [0] + order
-    for place, step in enumerate(steps):
-        lower(step)
-        if place:
-            raise_back(steps[place - 1])
-    raise_back(steps[-1])
-
-    for m in range(tensors - 1):
-        base_copies[m].wait_recv()
-        sq_copies[m].wait_recv()
-
     def give(step, src):
         def part(i, _):
             at = pl.ds(pl.multiple_of(i * mt, mt), mt)
@@ -342,14 +332,14 @@
 
         lax.fori_loop(0, rows // mt, part, 0)
 
-    for step in steps:
+    def settle(step):
         if step:
             ret_copies[step].wait_recv()
             give(step, ret_in.at[step])
         else:
             give(step, ret_out.at[step])
 
-    def finish(i, _):
+    def join(i, _):
         at = pl.ds(pl.multiple_of(i * tile, tile), tile)
         square = sq_out[at, :]
         total = acc[at, :]
@@ -357,7 +347,30 @@
             square = square + sq_in[m, at, :]
             total = total + base_in[m, at, :].astype(jnp.float32)
         mean = jnp.sum(square, axis=1, keepdims=True) / (width * tensors)
-        total = total * lax.rsqrt(mean + epsilon)
+        scale_t[at, :] = jnp.broadcast_to(lax.rsqrt(mean + epsilon), (tile, 128))
+        acc[at, :] = total
+        return 0
+
+    steps = [0] + order
+    lag = 3
+    for place, step in enumerate(steps):
+        lower(step)
+        if place:
+            raise_back(steps[place - 1])
+        if place >= lag:
+            settle(steps[place - lag])
+        if place == stores - 2:
+            for m in range(tensors - 1):
+                base_copies[m].wait_recv()
+                sq_copies[m].wait_recv()
+            lax.fori_loop(0, rows // tile, join, 0)
+    raise_back(steps[-1])
+    for step in steps[-lag:]:
+        settle(step)
+
+    def finish(i, _):
+        at = pl.ds(pl.multiple_of(i * tile, tile), tile)
+        total = acc[at, :] * scale_t[at, 0:1]
         c = cos_t[at, :]
         s = sin_t[at, :]
         for head in range(kv_local // HEAD):
@@ -408,6 +421,7 @@
             pltpu.VMEM((rows, 128), jnp.int32),
             pltpu.VMEM((rows, HEAD), f32),
             pltpu.VMEM((rows, HEAD), f32),
+            pltpu.VMEM((rows, 128), f32),
             pltpu.VMEM((rows, width), bf16),
             pltpu.VMEM((width, 2, kv_local * tensors), bf16),
             pltpu.VMEM((width, 2 * kv_local * tensors), bf16),

time: 170 us -> 178 us (1.047)
  the two profiles are of different devices: /device:TPU:17 before, /device:TPU:0 now
where the time goes in v3:
time: 178 us
  Pallas kernels  175 us (98%)
  local copies, waits for them, and re-layouts  2.23 us (1%)
    pallas_call x1, Pallas kernels, fused(): pl.pallas_call(functools.partial(fused_kernel, stores, tensors), out_shap...  175 us

profile of v3, /device:TPU:0, one launch (start us, length us, event | category | flops | bytes accessed | tf_op | source)
XLA Modules:
  0.0 177.8 jit_solution(4881139565640128359)
XLA Ops:
  0.6 174.9 %shard_map.95 = bf16[1024,512]{1,0:T(8,128)(2,1)} custom-call(bf16[1024,2048]{1,0:T(8,128)(2,1)} %tok.1, f32[1,2048]{1,0:T(1,128)} %bitcast.2, s32[1,1024]{1,0:T(1,128)} %bitcast.3, s32[32]{0:T(128)} %slots.1, s32[16]{0:T(128)} %lengths.1, bf16[4,2,64,256]{3,2,1,0:T(8,128)(2,1)} %up.1, bf16[2048,2,1024]{2,1,0:T(2,128)(2,1)} %w_hbm.1, ...), custom_call_target="tpu_custom_call" | custom-call | tf_op jit(solution)/shard_map/pallas_call | solution.py:414
  175.6 2.2 %fusion = (bf16[1024,256]{1,0:T(8,128)(2,1)}, bf16[1024,256]{1,0:T(8,128)(2,1)}) fusion(bf16[1024,512]{1,0:T(8,128)(2,1)} %shard_map.95), kind=kLoop, calls=%fused_computation | loop fusion | bytes 2097152 | tf_op jit(solution)/shard_map/slice | solution.py:465

commit v4 on v3

--- a/solution.py
+++ b/solution.py
@@ -352,20 +352,17 @@
         return 0
 
     steps = [0] + order
-    lag = 3
     for place, step in enumerate(steps):
         lower(step)
         if place:
             raise_back(steps[place - 1])
-        if place >= lag:
-            settle(steps[place - lag])
         if place == stores - 2:
             for m in range(tensors - 1):
                 base_copies[m].wait_recv()
                 sq_copies[m].wait_recv()
             lax.fori_loop(0, rows // tile, join, 0)
     raise_back(steps[-1])
-    for step in steps[-lag:]:
+    for step in steps:
         settle(step)
 
     def finish(i, _):

time: 178 us -> 170 us (0.955)
  the two profiles are of different devices: /device:TPU:0 before, /device:TPU:17 now
where the time goes in v4:
time: 170 us
  Pallas kernels  167 us (98%)
  local copies, waits for them, and re-layouts  2.23 us (1%)
    pallas_call x1, Pallas kernels, fused(): pl.pallas_call(functools.partial(fused_kernel, stores, tensors), out_shap...  167 us

profile of v4, /device:TPU:17, one launch (start us, length us, event | category | flops | bytes accessed | tf_op | source)
XLA Modules:
  0.0 170.1 jit_solution(9385860491603765645)
XLA Ops:
  0.6 167.2 %shard_map.95 = bf16[1024,512]{1,0:T(8,128)(2,1)} custom-call(bf16[1024,2048]{1,0:T(8,128)(2,1)} %tok.1, f32[1,2048]{1,0:T(1,128)} %bitcast.2, s32[1,1024]{1,0:T(1,128)} %bitcast.3, s32[32]{0:T(128)} %slots.1, s32[16]{0:T(128)} %lengths.1, bf16[4,2,64,256]{3,2,1,0:T(8,128)(2,1)} %up.1, bf16[2048,2,1024]{2,1,0:T(2,128)(2,1)} %w_hbm.1, ...), custom_call_target="tpu_custom_call" | custom-call | tf_op jit(solution)/shard_map/pallas_call | solution.py:411
  167.9 2.2 %fusion = (bf16[1024,256]{1,0:T(8,128)(2,1)}, bf16[1024,256]{1,0:T(8,128)(2,1)}) fusion(bf16[1024,512]{1,0:T(8,128)(2,1)} %shard_map.95), kind=kLoop, calls=%fused_computation | loop fusion | bytes 2097152 | tf_op jit(solution)/shard_map/slice | solution.py:462
